TPU v7x, 32 devices: a whole 2x2x4 slice. The times are simulated.
32 devices in a mesh: frame: 4 (over y, x), row: 8 (over z, core).
Axes of the slice: x: 2, y: 2, z: 4, core: 2. Of those that a mesh axis runs over, the one named last changes fastest.
Arguments:
- frames_in: bfloat16 [8, 32, 32, 256], P('frame', 'row'), may hold values from -6 to 6
- conv_first: bfloat16 [3, 3, 256, 256], replicated, may hold values from -0.125 to 0.125
- conv_second: bfloat16 [3, 3, 256, 256], replicated, may hold values from -0.125 to 0.125
- time_kernel: bfloat16 [3, 256, 256], replicated, may hold values from -0.21875 to 0.21875
- norm_gain: float32 [256], replicated, may hold values from 0.1 to 1.9
- w_query: bfloat16 [256, 256], replicated, may hold values from -0.375 to 0.375
- w_key: bfloat16 [256, 256], replicated, may hold values from -0.375 to 0.375
- w_value: bfloat16 [256, 256], replicated, may hold values from -0.375 to 0.375
- w_out: bfloat16 [256, 256], replicated, may hold values from -0.375 to 0.375
- frame_bias: float32 [8, 8], replicated, may hold values from -6 to 400
- conv_third: bfloat16 [3, 3, 256, 256], replicated, may hold values from -0.125 to 0.125
Outputs:
- encoded: bfloat16 [8, 32, 32, 256], P(None, 'row', 'frame')
All inputs are finite; a program needn't handle non-finite values.
Results may differ from a plain program's by a relative error of at most 0.018.
Values may be sent and summed in bfloat16 or wider, within the bound.
A program may use at most 64 MiB of HBM per device.

v0:
```python
import math
import jax
import jax.numpy as jnp
from jax import lax
from jax.sharding import PartitionSpec as P


def extended(cells, sides, width):
    for axis, dim in sides:
        count = lax.axis_size(axis)
        ends = count - 1
        head = lax.slice_in_dim(cells, 0, width, axis=dim)
        tail = lax.slice_in_dim(cells, cells.shape[dim] - width, cells.shape[dim], axis=dim)
        cells = jnp.concatenate(
            [
                lax.ppermute(tail, axis, [(i, (i + 1) % count) for i in range(ends)]),
                cells,
                lax.ppermute(head, axis, [((i + 1) % count, i) for i in range(ends)]),
            ],
            axis=dim,
        )
    return cells


def spatial(padded, weight, row_count, col_count):
    channels = weight.shape[2]
    summed = jnp.zeros((padded.shape[0] * row_count * col_count, weight.shape[3]), jnp.float32)
    for row_tap in range(3):
        for col_tap in range(3):
            window = padded[:, row_tap : row_tap + row_count, col_tap : col_tap + col_count, :]
            summed = summed + jnp.dot(
                window.reshape(-1, channels),
                weight[row_tap, col_tap],
                preferred_element_type=jnp.float32,
            )
    return summed.reshape(padded.shape[0], row_count, col_count, weight.shape[3])


def pad_columns(field):
    return jnp.pad(field, ((0, 0), (0, 0), (1, 1), (0, 0)))


def temporal(moved, time_kernel, norm_gain, w_query, w_key, w_value, w_out, frame_bias):
    frame_count = moved.shape[0]
    channels = moved.shape[-1]
    pixels = moved.reshape(frame_count, -1, channels)
    padded = jnp.pad(pixels, ((1, 1), (0, 0), (0, 0)))
    summed = pixels.astype(jnp.float32)
    for tap in range(3):
        shifted = padded[tap : tap + frame_count].reshape(-1, channels)
        summed = summed + jnp.dot(
            shifted, time_kernel[tap], preferred_element_type=jnp.float32
        ).reshape(pixels.shape)
    timed = summed.astype(jnp.bfloat16)
    widened = timed.astype(jnp.float32)
    scale_inv = lax.rsqrt(jnp.mean(widened * widened, axis=-1, keepdims=True) + 1e-06)
    normed = (widened * scale_inv * norm_gain).astype(jnp.bfloat16).reshape(-1, channels)
    queries = (
        jnp.dot(normed, w_query, preferred_element_type=jnp.float32)
        .astype(jnp.bfloat16)
        .reshape(pixels.shape)
    )
    key_rows = (
        jnp.dot(normed, w_key, preferred_element_type=jnp.float32)
        .astype(jnp.bfloat16)
        .reshape(pixels.shape)
    )
    value_rows = (
        jnp.dot(normed, w_value, preferred_element_type=jnp.float32)
        .astype(jnp.bfloat16)
        .reshape(pixels.shape)
    )
    scores = jnp.einsum(
        "fpc,gpc->pfg", queries, key_rows, preferred_element_type=jnp.float32
    ) / math.sqrt(channels)
    scores = scores + frame_bias
    peak = jnp.max(scores, axis=-1, keepdims=True)
    raised = jnp.exp(scores - peak)
    probs = (raised / jnp.sum(raised, axis=-1, keepdims=True)).astype(jnp.bfloat16)
    context = jnp.einsum(
        "pfg,gpc->fpc", probs, value_rows, preferred_element_type=jnp.float32
    ).astype(jnp.bfloat16)
    projected = jnp.dot(
        context.reshape(-1, channels), w_out, preferred_element_type=jnp.float32
    ).reshape(pixels.shape)
    return (widened + projected).astype(jnp.bfloat16).reshape(moved.shape)


def on_device(
    frames_in,
    conv_first,
    conv_second,
    time_kernel,
    norm_gain,
    w_query,
    w_key,
    w_value,
    w_out,
    frame_bias,
    conv_third,
):
    row_count = frames_in.shape[1]
    col_whole = frames_in.shape[2]
    haloed = extended(frames_in, (("row", 1),), 1)
    first = jax.nn.silu(spatial(pad_columns(haloed), conv_first, row_count, col_whole)).astype(
        jnp.bfloat16
    )
    haloed_two = extended(first, (("row", 1),), 1)
    second = jax.nn.silu(
        spatial(pad_columns(haloed_two), conv_second, row_count, col_whole)
    ).astype(jnp.bfloat16)
    moved = lax.all_to_all(second, "frame", split_axis=2, concat_axis=0, tiled=True)
    attended = temporal(moved, time_kernel, norm_gain, w_query, w_key, w_value, w_out, frame_bias)
    col_count = attended.shape[2]
    framed_last = extended(attended, (("frame", 2), ("row", 1)), 1)
    return spatial(framed_last, conv_third, row_count, col_count).astype(jnp.bfloat16)


def solution(mesh):
    placed = (P("frame", "row", None, None), P(), P(), P(), P(), P(), P(), P(), P(), P(), P())
    return jax.shard_map(
        on_device,
        mesh=mesh,
        in_specs=placed,
        out_specs=P(None, "row", "frame", None),
        check_vma=False,
    )
```

profile of v0, /device:TPU:21, one launch (start us, length us, event | category | flops | bytes accessed | tf_op | source)
XLA Modules:
  0.0 54.3 jit_solution(5470945481003135327)
XLA Ops:
  0.0 0.9 %fusion.102 = (bf16[2,1,32,256]{3,2,1,0:T(8,128)(2,1)S(1)}, bf16[2,1,32,256]{3,2,1,0:T(8,128)(2,1)S(1)}) fusion(bf16[2,4,32,256]{3,2,1,0:T(8,128)(2,1)} %param.11), kind=kLoop, calls=%fused_computation.152 | loop fusion | bytes 131072 | tf_op jit(solution)/shard_map/slice | solution.py:13
  0.9 2.6 %collective-permute-start.1 = (bf16[2,1,32,256]{3,2,1,0:T(8,128)(2,1)S(1)}, bf16[2,1,32,256]{3,2,1,0:T(8,128)(2,1)S(1)}, u32[]{:S(2)}, u32[]{:S(2)}) collective-permute-start(bf16[2,1,32,256]{3,2,1,0:T(8,128)(2,1)S(1)} %get-tuple-element.38), channel_id=1, source_target_pairs={{1,0},{2,1},{3,2},{4,3},{5,4},{6,5},{7,6},{9,8},{10,9},{11,10},{12... | collective-permute-start | bytes 98312 | tf_op jit(solution)/shard_map/ppermute | solution.py:18
  3.5 3.1 %collective-permute-start = (bf16[2,1,32,256]{3,2,1,0:T(8,128)(2,1)S(1)}, bf16[2,1,32,256]{3,2,1,0:T(8,128)(2,1)S(1)}, u32[]{:S(2)}, u32[]{:S(2)}) collective-permute-start(bf16[2,1,32,256]{3,2,1,0:T(8,128)(2,1)S(1)} %get-tuple-element.37), channel_id=1, source_target_pairs={{0,1},{1,2},{2,3},{3,4},{4,5},{5,6},{6,7},{8,9},{9,10},{10,11},{11... | collective-permute-start | bytes 98312 | tf_op jit(solution)/shard_map/ppermute | solution.py:16
  6.6 1.0 %collective-permute-done = bf16[2,1,32,256]{3,2,1,0:T(8,128)(2,1)S(1)} collective-permute-done((bf16[2,1,32,256]{3,2,1,0:T(8,128)(2,1)S(1)}, bf16[2,1,32,256]{3,2,1,0:T(8,128)(2,1)S(1)}, u32[]{:S(2)}, u32[]{:S(2)}) %collective-permute-start) | collective-permute-done | bytes 32800 | tf_op jit(solution)/shard_map/ppermute | solution.py:16
  7.6 1.0 %fusion.19 = bf16[2,6,34,256]{3,2,1,0:T(8,128)(2,1)S(1)} fusion(bf16[2,1,32,256]{3,2,1,0:T(8,128)(2,1)S(1)} %collective-permute-done.1, bf16[2,4,32,256]{3,2,1,0:T(8,128)(2,1)} %param.11, bf16[2,1,32,256]{3,2,1,0:T(8,128)(2,1)S(1)} %collective-permute-done), kind=kLoop, calls=%fused_computation.58 | loop fusion | flops 1253376 | bytes 405504 | tf_op jit(solution)/shard_map/concatenate | solution.py:14
  9.1 0.4 copy-done.1
  9.5 0.2 convolution_add_fusion.22
  10.1 0.2 convolution_add_fusion.19
  11.0 3.2 %collective-permute-start.3 = (bf16[2,1,32,256]{3,2,1,0:T(8,128)(2,1)S(1)}, bf16[2,1,32,256]{3,2,1,0:T(8,128)(2,1)S(1)}, u32[]{:S(2)}, u32[]{:S(2)}) collective-permute-start(bf16[2,1,32,256]{3,2,1,0:T(8,128)(2,1)S(1)} %get-tuple-element.34), channel_id=1, source_target_pairs={{1,0},{2,1},{3,2},{4,3},{5,4},{6,5},{7,6},{9,8},{10,9},{11,10},{12... | collective-permute-start | bytes 98312 | tf_op jit(solution)/shard_map/ppermute | solution.py:18
  14.2 3.1 %collective-permute-start.2 = (bf16[2,1,32,256]{3,2,1,0:T(8,128)(2,1)S(1)}, bf16[2,1,32,256]{3,2,1,0:T(8,128)(2,1)S(1)}, u32[]{:S(2)}, u32[]{:S(2)}) collective-permute-start(bf16[2,1,32,256]{3,2,1,0:T(8,128)(2,1)S(1)} %get-tuple-element.33), channel_id=1, source_target_pairs={{0,1},{1,2},{2,3},{3,4},{4,5},{5,6},{6,7},{8,9},{9,10},{10,11},{11... | collective-permute-start | bytes 98312 | tf_op jit(solution)/shard_map/ppermute | solution.py:16
  17.3 1.0 %collective-permute-done.2 = bf16[2,1,32,256]{3,2,1,0:T(8,128)(2,1)S(1)} collective-permute-done((bf16[2,1,32,256]{3,2,1,0:T(8,128)(2,1)S(1)}, bf16[2,1,32,256]{3,2,1,0:T(8,128)(2,1)S(1)}, u32[]{:S(2)}, u32[]{:S(2)}) %collective-permute-start.2) | collective-permute-done | bytes 32800 | tf_op jit(solution)/shard_map/ppermute | solution.py:16
  18.9 0.2 convolution_add_fusion.15
  19.5 0.2 convolution_add_fusion.12
  19.7 0.2 convolution_add_fusion.11
  20.4 0.8 %copy.24 = bf16[2,4,32,256]{3,1,0,2:T(4,128)(2,1)} copy(bf16[2,4,32,256]{3,2,1,0:T(8,128)(2,1)S(1)} %multiply_convert_fusion.1) | data formatting | bytes 262144 | tf_op jit(solution)/shard_map/convert_element_type | solution.py:111
  21.1 3.7 %all-to-all-start = ((bf16[2,4,32,256]{3,1,0,2:T(4,128)(2,1)}), bf16[2,4,32,256]{3,1,0,2:T(4,128)(2,1)S(1)}, u32[]{:S(2)}, u32[]{:S(2)}) async-start(bf16[2,4,32,256]{3,1,0,2:T(4,128)(2,1)} %copy.24), calls=%async_computation | async-start | bytes 262144 | tf_op jit(solution)/shard_map/all_to_all | solution.py:112
  24.9 3.3 %all-to-all-done = bf16[2,4,32,256]{3,1,0,2:T(4,128)(2,1)S(1)} async-done(((bf16[2,4,32,256]{3,1,0,2:T(4,128)(2,1)}), bf16[2,4,32,256]{3,1,0,2:T(4,128)(2,1)S(1)}, u32[]{:S(2)}, u32[]{:S(2)}) %all-to-all-start) | async-done | bytes 131104 | tf_op jit(solution)/shard_map/all_to_all | solution.py:112
  28.4 0.2 fusion.1
  28.6 0.3 multiply_reduce_fusion
  29.7 0.3 fusion.13
  30.0 0.3 fusion.11
  30.6 2.8 %collective-permute-start.5 = (bf16[8,4,1,256]{3,2,1,0:T(2,128)(2,1)S(1)}, bf16[8,4,1,256]{3,2,1,0:T(2,128)(2,1)S(1)}, u32[]{:S(2)}, u32[]{:S(2)}) collective-permute-start(bf16[8,4,1,256]{3,2,1,0:T(2,128)(2,1)S(1)} %get-tuple-element.30), channel_id=1, source_target_pairs={{8,0},{16,8},{24,16},{9,1},{17,9},{25,17},{10,2},{18,10},{26,18},{... | collective-permute-start | bytes 49160 | tf_op jit(solution)/shard_map/ppermute | solution.py:18
  33.4 2.5 %collective-permute-start.4 = (bf16[8,4,1,256]{3,2,1,0:T(2,128)(2,1)S(1)}, bf16[8,4,1,256]{3,2,1,0:T(2,128)(2,1)S(1)}, u32[]{:S(2)}, u32[]{:S(2)}) collective-permute-start(bf16[8,4,1,256]{3,2,1,0:T(2,128)(2,1)S(1)} %get-tuple-element.29), channel_id=1, source_target_pairs={{0,8},{8,16},{16,24},{1,9},{9,17},{17,25},{2,10},{10,18},{18,26},{... | collective-permute-start | bytes 49160 | tf_op jit(solution)/shard_map/ppermute | solution.py:16
  36.1 2.9 %collective-permute-done.4 = bf16[8,4,1,256]{3,2,1,0:T(2,128)(2,1)S(1)} collective-permute-done((bf16[8,4,1,256]{3,2,1,0:T(2,128)(2,1)S(1)}, bf16[8,4,1,256]{3,2,1,0:T(2,128)(2,1)S(1)}, u32[]{:S(2)}, u32[]{:S(2)}) %collective-permute-start.4) | collective-permute-done | bytes 16416 | tf_op jit(solution)/shard_map/ppermute | solution.py:16
  39.0 7.1 %collective-permute-start.6 = (bf16[8,1,10,256]{3,2,1,0:T(8,128)(2,1)S(1)}, bf16[8,1,10,256]{3,2,1,0:T(8,128)(2,1)S(1)}, u32[]{:S(2)}, u32[]{:S(2)}) collective-permute-start(bf16[8,1,10,256]{3,2,1,0:T(8,128)(2,1)S(1)} %get-tuple-element.25), channel_id=1, source_target_pairs={{0,1},{1,2},{2,3},{3,4},{4,5},{5,6},{6,7},{8,9},{9,10},{10,11},{11... | collective-permute-start | bytes 122888 | tf_op jit(solution)/shard_map/ppermute | solution.py:16
  46.1 1.9 %collective-permute-start.7 = (bf16[8,1,10,256]{3,2,1,0:T(8,128)(2,1)S(1)}, bf16[8,1,10,256]{3,2,1,0:T(8,128)(2,1)S(1)}, u32[]{:S(2)}, u32[]{:S(2)}) collective-permute-start(bf16[8,1,10,256]{3,2,1,0:T(8,128)(2,1)S(1)} %get-tuple-element.26), channel_id=1, source_target_pairs={{1,0},{2,1},{3,2},{4,3},{5,4},{6,5},{7,6},{9,8},{10,9},{11,10},{12... | collective-permute-start | bytes 122888 | tf_op jit(solution)/shard_map/ppermute | solution.py:18
  48.2 3.5 %collective-permute-done.7 = bf16[8,1,10,256]{3,2,1,0:T(8,128)(2,1)S(1)} collective-permute-done((bf16[8,1,10,256]{3,2,1,0:T(8,128)(2,1)S(1)}, bf16[8,1,10,256]{3,2,1,0:T(8,128)(2,1)S(1)}, u32[]{:S(2)}, u32[]{:S(2)}) %collective-permute-start.7) | collective-permute-done | bytes 40992 | tf_op jit(solution)/shard_map/ppermute | solution.py:18
  51.7 0.3 maximum_maximum_fusion
  52.5 0.2 convolution_add_fusion.7
  52.9 0.2 fusion.3
  53.1 0.2 fusion.2
  53.5 0.8 %fusion.7 = bf16[256,256]{1,0:T(8,128)(2,1)} fusion(f32[256,256]{1,0:T(8,128)S(1)} %convolution_add_fusion.3, bf16[256,256]{1,0:T(8,128)(2,1)S(1)} %bitcast.189, bf16[3,3,256,256]{3,2,1,0:T(8,128)(2,1)S(1)} %copy-done.3), kind=kOutput, calls=%fused_computation.30 | convolution fusion | flops 33685504 | bytes 655360 | tf_op jit(solution)/shard_map/dot_general | solution.py:31
  (65 shorter events, 5.6 us)
Async XLA Ops:
  0.0 29.0 %copy-start = (bf16[256,256]{1,0:T(8,128)(2,1)S(1)}, bf16[256,256]{1,0:T(8,128)(2,1)}, u32[]{:S(2)}) copy-start(bf16[256,256]{1,0:T(8,128)(2,1)} %param.18) | copy-start | bytes 393220
  0.0 8.7 %copy-start.2 = (bf16[3,3,256,256]{3,2,1,0:T(8,128)(2,1)S(1)}, bf16[3,3,256,256]{3,2,1,0:T(8,128)(2,1)}, u32[]{:S(2)}) copy-start(bf16[3,3,256,256]{3,2,1,0:T(8,128)(2,1)} %param.12) | copy-start | bytes 3538948
  0.9 5.7 %collective-permute-start.1 = (bf16[2,1,32,256]{3,2,1,0:T(8,128)(2,1)S(1)}, bf16[2,1,32,256]{3,2,1,0:T(8,128)(2,1)S(1)}, u32[]{:S(2)}, u32[]{:S(2)}) collective-permute-start(bf16[2,1,32,256]{3,2,1,0:T(8,128)(2,1)S(1)} %get-tuple-element.38), channel_id=1, source_target_pairs={{1,0},{2,1},{3,2},{4,3},{5,4},{6,5},{7,6},{9,8},{10,9},{11,10},{12... | collective-permute-start | bytes 98312 | tf_op jit(solution)/shard_map/ppermute | solution.py:18
  3.5 4.1 %collective-permute-start = (bf16[2,1,32,256]{3,2,1,0:T(8,128)(2,1)S(1)}, bf16[2,1,32,256]{3,2,1,0:T(8,128)(2,1)S(1)}, u32[]{:S(2)}, u32[]{:S(2)}) collective-permute-start(bf16[2,1,32,256]{3,2,1,0:T(8,128)(2,1)S(1)} %get-tuple-element.37), channel_id=1, source_target_pairs={{0,1},{1,2},{2,3},{3,4},{4,5},{5,6},{6,7},{8,9},{9,10},{10,11},{11... | collective-permute-start | bytes 98312 | tf_op jit(solution)/shard_map/ppermute | solution.py:16
  8.6 0.9 %copy-start.1 = (bf16[2,4,32,256]{3,2,1,0:T(8,128)(2,1)S(1)}, bf16[2,4,32,256]{3,2,1,0:T(8,128)(2,1)}, u32[]{:S(2)}) copy-start(bf16[2,4,32,256]{3,2,1,0:T(8,128)(2,1)} %param.11) | copy-start | bytes 393220
  10.9 7.6 %copy-start.4 = (bf16[3,3,256,256]{3,2,1,0:T(8,128)(2,1)S(1)}, bf16[3,3,256,256]{3,2,1,0:T(8,128)(2,1)}, u32[]{:S(2)}) copy-start(bf16[3,3,256,256]{3,2,1,0:T(8,128)(2,1)} %param.13) | copy-start | bytes 3538948
  11.0 6.3 %collective-permute-start.3 = (bf16[2,1,32,256]{3,2,1,0:T(8,128)(2,1)S(1)}, bf16[2,1,32,256]{3,2,1,0:T(8,128)(2,1)S(1)}, u32[]{:S(2)}, u32[]{:S(2)}) collective-permute-start(bf16[2,1,32,256]{3,2,1,0:T(8,128)(2,1)S(1)} %get-tuple-element.34), channel_id=1, source_target_pairs={{1,0},{2,1},{3,2},{4,3},{5,4},{6,5},{7,6},{9,8},{10,9},{11,10},{12... | collective-permute-start | bytes 98312 | tf_op jit(solution)/shard_map/ppermute | solution.py:18
  14.2 4.1 %collective-permute-start.2 = (bf16[2,1,32,256]{3,2,1,0:T(8,128)(2,1)S(1)}, bf16[2,1,32,256]{3,2,1,0:T(8,128)(2,1)S(1)}, u32[]{:S(2)}, u32[]{:S(2)}) collective-permute-start(bf16[2,1,32,256]{3,2,1,0:T(8,128)(2,1)S(1)} %get-tuple-element.33), channel_id=1, source_target_pairs={{0,1},{1,2},{2,3},{3,4},{4,5},{5,6},{6,7},{8,9},{9,10},{10,11},{11... | collective-permute-start | bytes 98312 | tf_op jit(solution)/shard_map/ppermute | solution.py:16
  20.1 4.7 %copy-start.9 = (f32[8,8]{1,0:T(8,128)S(1)}, f32[8,8]{1,0:T(8,128)}, u32[]{:S(2)}) copy-start(f32[8,8]{1,0:T(8,128)} %param.20) | copy-start | bytes 772
  20.1 8.1 %copy-start.5 = (bf16[3,256,256]{2,1,0:T(8,128)(2,1)S(1)}, bf16[3,256,256]{2,1,0:T(8,128)(2,1)}, u32[]{:S(2)}) copy-start(bf16[3,256,256]{2,1,0:T(8,128)(2,1)} %param.14) | copy-start | bytes 1179652
  21.1 7.0 %all-to-all-start = ((bf16[2,4,32,256]{3,1,0,2:T(4,128)(2,1)}), bf16[2,4,32,256]{3,1,0,2:T(4,128)(2,1)S(1)}, u32[]{:S(2)}, u32[]{:S(2)}) async-start(bf16[2,4,32,256]{3,1,0,2:T(4,128)(2,1)} %copy.24), calls=%async_computation | async-start | bytes 262144 | tf_op jit(solution)/shard_map/all_to_all | solution.py:112
  28.1 0.7 %copy-start.10 = (f32[256]{0:T(256)S(1)}, f32[256]{0:T(256)}, u32[]{:S(2)}) copy-start(f32[256]{0:T(256)} %param.15) | copy-start | bytes 3076
  28.4 0.9 %copy-start.6 = (bf16[256,256]{1,0:T(8,128)(2,1)S(1)}, bf16[256,256]{1,0:T(8,128)(2,1)}, u32[]{:S(2)}) copy-start(bf16[256,256]{1,0:T(8,128)(2,1)} %param.17) | copy-start | bytes 393220
  28.6 0.9 %copy-start.7 = (bf16[256,256]{1,0:T(8,128)(2,1)S(1)}, bf16[256,256]{1,0:T(8,128)(2,1)}, u32[]{:S(2)}) copy-start(bf16[256,256]{1,0:T(8,128)(2,1)} %param.16) | copy-start | bytes 393220
  29.3 1.0 %copy-start.8 = (bf16[256,256]{1,0:T(8,128)(2,1)S(1)}, bf16[256,256]{1,0:T(8,128)(2,1)}, u32[]{:S(2)}) copy-start(bf16[256,256]{1,0:T(8,128)(2,1)} %param.19) | copy-start | bytes 393220
  29.7 6.2 %copy-start.3 = (bf16[3,3,256,256]{3,2,1,0:T(8,128)(2,1)S(1)}, bf16[3,3,256,256]{3,2,1,0:T(8,128)(2,1)}, u32[]{:S(2)}) copy-start(bf16[3,3,256,256]{3,2,1,0:T(8,128)(2,1)} %param.21) | copy-start | bytes 3538948
  30.6 5.5 %collective-permute-start.5 = (bf16[8,4,1,256]{3,2,1,0:T(2,128)(2,1)S(1)}, bf16[8,4,1,256]{3,2,1,0:T(2,128)(2,1)S(1)}, u32[]{:S(2)}, u32[]{:S(2)}) collective-permute-start(bf16[8,4,1,256]{3,2,1,0:T(2,128)(2,1)S(1)} %get-tuple-element.30), channel_id=1, source_target_pairs={{8,0},{16,8},{24,16},{9,1},{17,9},{25,17},{10,2},{18,10},{26,18},{... | collective-permute-start | bytes 49160 | tf_op jit(solution)/shard_map/ppermute | solution.py:18
  33.4 5.6 %collective-permute-start.4 = (bf16[8,4,1,256]{3,2,1,0:T(2,128)(2,1)S(1)}, bf16[8,4,1,256]{3,2,1,0:T(2,128)(2,1)S(1)}, u32[]{:S(2)}, u32[]{:S(2)}) collective-permute-start(bf16[8,4,1,256]{3,2,1,0:T(2,128)(2,1)S(1)} %get-tuple-element.29), channel_id=1, source_target_pairs={{0,8},{8,16},{16,24},{1,9},{9,17},{17,25},{2,10},{10,18},{18,26},{... | collective-permute-start | bytes 49160 | tf_op jit(solution)/shard_map/ppermute | solution.py:16
  39.0 9.2 %collective-permute-start.6 = (bf16[8,1,10,256]{3,2,1,0:T(8,128)(2,1)S(1)}, bf16[8,1,10,256]{3,2,1,0:T(8,128)(2,1)S(1)}, u32[]{:S(2)}, u32[]{:S(2)}) collective-permute-start(bf16[8,1,10,256]{3,2,1,0:T(8,128)(2,1)S(1)} %get-tuple-element.25), channel_id=1, source_target_pairs={{0,1},{1,2},{2,3},{3,4},{4,5},{5,6},{6,7},{8,9},{9,10},{10,11},{11... | collective-permute-start | bytes 122888 | tf_op jit(solution)/shard_map/ppermute | solution.py:16
  46.1 5.6 %collective-permute-start.7 = (bf16[8,1,10,256]{3,2,1,0:T(8,128)(2,1)S(1)}, bf16[8,1,10,256]{3,2,1,0:T(8,128)(2,1)S(1)}, u32[]{:S(2)}, u32[]{:S(2)}) collective-permute-start(bf16[8,1,10,256]{3,2,1,0:T(8,128)(2,1)S(1)} %get-tuple-element.26), channel_id=1, source_target_pairs={{1,0},{2,1},{3,2},{4,3},{5,4},{6,5},{7,6},{9,8},{10,9},{11,10},{12... | collective-permute-start | bytes 122888 | tf_op jit(solution)/shard_map/ppermute | solution.py:18
where the time goes:
time: 54.8 us; the launch traced here: 54.3 us
  starting transfers between devices  29.9 us (55%)
  waiting for transfers between devices  11.6 us (21%)
  matrix products  7.61 us (14%)
  local copies, waits for them, and re-layouts  2.71 us (5%)
  other arithmetic  1.94 us (4%)
  between operations  0.57 us (1%)
    ppermute x4, starting transfers between devices, extended(): lax.ppermute(tail, axis, [(i, (i + 1) % count) for i in range(ends)])  15.8 us
    ppermute x4, starting transfers between devices, extended(): lax.ppermute(head, axis, [((i + 1) % count, i) for i in range(ends)])  10.5 us
    dot_general x27, matrix products, spatial(): jnp.dot(window.reshape(-1, channels), weight[row_tap, col_tap], preferred...  5.71 us
    ppermute x4, waiting for transfers between devices, extended(): lax.ppermute(tail, axis, [(i, (i + 1) % count) for i in range(ends)])  4.84 us
    all_to_all x1, starting transfers between devices, on_device(): lax.all_to_all(second, 'frame', split_axis=2, concat_axis=0, tiled=True)  3.67 us
    ppermute x4, waiting for transfers between devices, extended(): lax.ppermute(head, axis, [((i + 1) % count, i) for i in range(ends)])  3.52 us
    all_to_all x1, waiting for transfers between devices, on_device(): lax.all_to_all(second, 'frame', split_axis=2, concat_axis=0, tiled=True)  3.27 us
    concatenate x6, other arithmetic, extended(): jnp.concatenate([lax.ppermute(tail, axis, [(i, (i + 1) % count) for i in...  1.53 us
  transfers between devices with their start and end apart: 9, of which 5 were waited for; matrix products, arithmetic and copies ran while one was open for 1% of the time, Pallas kernels for 0%

commit v1 on v0

--- a/solution.py
+++ b/solution.py
@@ -109,7 +109,27 @@
     second = jax.nn.silu(
         spatial(pad_columns(haloed_two), conv_second, row_count, col_whole)
     ).astype(jnp.bfloat16)
-    moved = lax.all_to_all(second, "frame", split_axis=2, concat_axis=0, tiled=True)
+
+    def wait_rails(row_dim, across, axis_no, arr_in):
+        v_next, res = (lax.axis_size(across), lax.axis_index(across))
+        low = arr_in.shape[row_dim] // v_next
+        mixed_arr = list(arr_in.shape)
+        mixed_arr[row_dim] = low
+        row_out = mixed_arr[axis_no]
+        mixed_arr[axis_no] = row_out * v_next
+        local_out = jnp.zeros(mixed_arr, arr_in.dtype)
+        for tick in [*range(v_next)]:
+            k_now = lax.dynamic_slice_in_dim(arr_in, (res ^ tick) * low, low, axis=row_dim)
+            if tick:
+                k_now = lax.ppermute(
+                    k_now, across, [(hop_no, hop_no ^ tick) for hop_no in range(v_next)]
+                )
+            local_out = lax.dynamic_update_slice_in_dim(
+                local_out, k_now, (res ^ tick) * row_out, axis=axis_no
+            )
+        return local_out
+
+    moved = wait_rails(2, "frame", 0, second)
     attended = temporal(moved, time_kernel, norm_gain, w_query, w_key, w_value, w_out, frame_bias)
     col_count = attended.shape[2]
     framed_last = extended(attended, (("frame", 2), ("row", 1)), 1)

time: 54.8 us -> 52.8 us (0.964)
  starting transfers between devices: 29.9 us -> 28.7 us
  local copies, waits for them, and re-layouts: 2.71 us -> 1.96 us
    all_to_all x1 -> x0, starting transfers between devices: 3.67 us -> none  [on_device(): lax.all_to_all(second, 'frame', split_axis=2, concat_axis=0, tiled=True)]
    all_to_all x1 -> x0, waiting for transfers between devices: 3.27 us -> none  [on_device(): lax.all_to_all(second, 'frame', split_axis=2, concat_axis=0, tiled=True)]
    ppermute x0 -> x3, starting transfers between devices: none -> 2.71 us  [wait_rails(): lax.ppermute(k_now, across, [(hop_no, hop_no ^ tick) for hop_no in range(...]
    ppermute x0 -> x3, waiting for transfers between devices: none -> 2.43 us  [wait_rails(): lax.ppermute(k_now, across, [(hop_no, hop_no ^ tick) for hop_no in range(...]
    ppermute x4, starting transfers between devices: 15.8 us -> 14.9 us  [extended(): lax.ppermute(tail, axis, [(i, (i + 1) % count) for i in range(ends)])]
    ppermute x4, waiting for transfers between devices: 4.84 us -> 5.67 us  [extended(): lax.ppermute(tail, axis, [(i, (i + 1) % count) for i in range(ends)])]
    convert_element_type x1 -> x0, local copies, waits for them, and re-layouts: 0.76 us -> none  [on_device(): second = jax.nn.silu(spatial(pad_columns(haloed_two), conv_second, row_co...]
    ppermute x4, starting transfers between devices: 10.5 us -> 11.1 us  [extended(): lax.ppermute(head, axis, [((i + 1) % count, i) for i in range(ends)])]
  transfers between devices with their start and end apart: 9 -> 11, of which waited for: 5 -> 6; matrix products, arithmetic and copies ran while one was open for 1% -> 1% of each run, Pallas kernels for 0% -> 0%
where the time goes in v1:
time: 52.8 us; the launch traced here: 52.5 us
  starting transfers between devices  28.7 us (54%)
  waiting for transfers between devices  11.6 us (22%)
  matrix products  7.6 us (14%)
  local copies, waits for them, and re-layouts  1.96 us (4%)
  other arithmetic  1.94 us (4%)
  between operations  0.62 us (1%)
    ppermute x4, starting transfers between devices, extended(): lax.ppermute(tail, axis, [(i, (i + 1) % count) for i in range(ends)])  14.9 us
    ppermute x4, starting transfers between devices, extended(): lax.ppermute(head, axis, [((i + 1) % count, i) for i in range(ends)])  11.1 us
    dot_general x27, matrix products, spatial(): jnp.dot(window.reshape(-1, channels), weight[row_tap, col_tap], preferred...  5.72 us
    ppermute x4, waiting for transfers between devices, extended(): lax.ppermute(tail, axis, [(i, (i + 1) % count) for i in range(ends)])  5.67 us
    ppermute x4, waiting for transfers between devices, extended(): lax.ppermute(head, axis, [((i + 1) % count, i) for i in range(ends)])  3.52 us
    ppermute x3, starting transfers between devices, wait_rails(): lax.ppermute(k_now, across, [(hop_no, hop_no ^ tick) for hop_no in range(...  2.71 us
    ppermute x3, waiting for transfers between devices, wait_rails(): lax.ppermute(k_now, across, [(hop_no, hop_no ^ tick) for hop_no in range(...  2.43 us
    concatenate x6, other arithmetic, extended(): jnp.concatenate([lax.ppermute(tail, axis, [(i, (i + 1) % count) for i in...  1.53 us
  transfers between devices with their start and end apart: 11, of which 6 were waited for; matrix products, arithmetic and copies ran while one was open for 1% of the time, Pallas kernels for 0%

profile of v1, /device:TPU:21, one launch (start us, length us, event | category | flops | bytes accessed | tf_op | source)
XLA Modules:
  0.0 52.5 jit_solution(11993837005561786987)
XLA Ops:
  0.0 0.9 %fusion.110 = (bf16[2,1,32,256]{3,2,1,0:T(8,128)(2,1)S(1)}, bf16[2,1,32,256]{3,2,1,0:T(8,128)(2,1)S(1)}) fusion(bf16[2,4,32,256]{3,2,1,0:T(8,128)(2,1)} %param.11), kind=kLoop, calls=%fused_computation.163 | loop fusion | bytes 131072 | tf_op jit(solution)/shard_map/slice | solution.py:13
  0.9 2.6 %collective-permute-start.1 = (bf16[2,1,32,256]{3,2,1,0:T(8,128)(2,1)S(1)}, bf16[2,1,32,256]{3,2,1,0:T(8,128)(2,1)S(1)}, u32[]{:S(2)}, u32[]{:S(2)}) collective-permute-start(bf16[2,1,32,256]{3,2,1,0:T(8,128)(2,1)S(1)} %get-tuple-element.42), channel_id=1, source_target_pairs={{1,0},{2,1},{3,2},{4,3},{5,4},{6,5},{7,6},{9,8},{10,9},{11,10},{12... | collective-permute-start | bytes 98312 | tf_op jit(solution)/shard_map/ppermute | solution.py:18
  3.5 3.1 %collective-permute-start = (bf16[2,1,32,256]{3,2,1,0:T(8,128)(2,1)S(1)}, bf16[2,1,32,256]{3,2,1,0:T(8,128)(2,1)S(1)}, u32[]{:S(2)}, u32[]{:S(2)}) collective-permute-start(bf16[2,1,32,256]{3,2,1,0:T(8,128)(2,1)S(1)} %get-tuple-element.41), channel_id=1, source_target_pairs={{0,1},{1,2},{2,3},{3,4},{4,5},{5,6},{6,7},{8,9},{9,10},{10,11},{11... | collective-permute-start | bytes 98312 | tf_op jit(solution)/shard_map/ppermute | solution.py:16
  6.6 1.0 %collective-permute-done = bf16[2,1,32,256]{3,2,1,0:T(8,128)(2,1)S(1)} collective-permute-done((bf16[2,1,32,256]{3,2,1,0:T(8,128)(2,1)S(1)}, bf16[2,1,32,256]{3,2,1,0:T(8,128)(2,1)S(1)}, u32[]{:S(2)}, u32[]{:S(2)}) %collective-permute-start) | collective-permute-done | bytes 32800 | tf_op jit(solution)/shard_map/ppermute | solution.py:16
  7.6 1.0 %fusion.18 = bf16[2,6,34,256]{3,2,1,0:T(8,128)(2,1)S(1)} fusion(bf16[2,1,32,256]{3,2,1,0:T(8,128)(2,1)S(1)} %collective-permute-done.1, bf16[2,4,32,256]{3,2,1,0:T(8,128)(2,1)} %param.11, bf16[2,1,32,256]{3,2,1,0:T(8,128)(2,1)S(1)} %collective-permute-done), kind=kLoop, calls=%fused_computation.56 | loop fusion | flops 1253376 | bytes 405504 | tf_op jit(solution)/shard_map/concatenate | solution.py:14
  9.1 0.4 copy-done.1
  9.5 0.2 convolution_add_fusion.20
  11.0 3.2 %collective-permute-start.3 = (bf16[2,1,32,256]{3,2,1,0:T(8,128)(2,1)S(1)}, bf16[2,1,32,256]{3,2,1,0:T(8,128)(2,1)S(1)}, u32[]{:S(2)}, u32[]{:S(2)}) collective-permute-start(bf16[2,1,32,256]{3,2,1,0:T(8,128)(2,1)S(1)} %get-tuple-element.38), channel_id=1, source_target_pairs={{1,0},{2,1},{3,2},{4,3},{5,4},{6,5},{7,6},{9,8},{10,9},{11,10},{12... | collective-permute-start | bytes 98312 | tf_op jit(solution)/shard_map/ppermute | solution.py:18
  14.2 3.1 %collective-permute-start.2 = (bf16[2,1,32,256]{3,2,1,0:T(8,128)(2,1)S(1)}, bf16[2,1,32,256]{3,2,1,0:T(8,128)(2,1)S(1)}, u32[]{:S(2)}, u32[]{:S(2)}) collective-permute-start(bf16[2,1,32,256]{3,2,1,0:T(8,128)(2,1)S(1)} %get-tuple-element.37), channel_id=1, source_target_pairs={{0,1},{1,2},{2,3},{3,4},{4,5},{5,6},{6,7},{8,9},{9,10},{10,11},{11... | collective-permute-start | bytes 98312 | tf_op jit(solution)/shard_map/ppermute | solution.py:16
  17.3 1.0 %collective-permute-done.2 = bf16[2,1,32,256]{3,2,1,0:T(8,128)(2,1)S(1)} collective-permute-done((bf16[2,1,32,256]{3,2,1,0:T(8,128)(2,1)S(1)}, bf16[2,1,32,256]{3,2,1,0:T(8,128)(2,1)S(1)}, u32[]{:S(2)}, u32[]{:S(2)}) %collective-permute-start.2) | collective-permute-done | bytes 32800 | tf_op jit(solution)/shard_map/ppermute | solution.py:16
  18.9 0.2 convolution_add_fusion.13
  19.5 0.2 convolution_add_fusion.10
  19.7 0.2 convolution_add_fusion.9
  20.1 0.2 fusion.3
  20.5 1.3 %collective-permute-start.4 = (bf16[2,4,8,256]{3,2,1,0:T(8,128)(2,1)S(1)}, bf16[2,4,8,256]{3,2,1,0:T(8,128)(2,1)S(1)}, u32[]{:S(2)}, u32[]{:S(2)}) collective-permute-start(bf16[2,4,8,256]{3,2,1,0:T(8,128)(2,1)S(1)} %get-tuple-element.33), channel_id=1, source_target_pairs={{0,8},{8,0},{16,24},{24,16},{1,9},{9,1},{17,25},{25,17},{2,10},{10... | collective-permute-start | bytes 98312 | tf_op jit(solution)/shard_map/ppermute | solution.py:124
  21.8 0.2 collective-permute-start.5
  22.0 1.2 %collective-permute-start.6 = (bf16[2,4,8,256]{3,2,1,0:T(8,128)(2,1)S(1)}, bf16[2,4,8,256]{3,2,1,0:T(8,128)(2,1)S(1)}, u32[]{:S(2)}, u32[]{:S(2)}) collective-permute-start(bf16[2,4,8,256]{3,2,1,0:T(8,128)(2,1)S(1)} %get-tuple-element.31), channel_id=1, source_target_pairs={{0,24},{8,16},{16,8},{24,0},{1,25},{9,17},{17,9},{25,1},{2,26},{10... | collective-permute-start | bytes 98312 | tf_op jit(solution)/shard_map/ppermute | solution.py:124
  23.3 1.6 %collective-permute-done.5 = bf16[2,4,8,256]{3,2,1,0:T(8,128)(2,1)S(1)} collective-permute-done((bf16[2,4,8,256]{3,2,1,0:T(8,128)(2,1)S(1)}, bf16[2,4,8,256]{3,2,1,0:T(8,128)(2,1)S(1)}, u32[]{:S(2)}, u32[]{:S(2)}) %collective-permute-start.5) | collective-permute-done | bytes 32800 | tf_op jit(solution)/shard_map/ppermute | solution.py:124
  24.9 0.8 %collective-permute-done.6 = bf16[2,4,8,256]{3,2,1,0:T(8,128)(2,1)S(1)} collective-permute-done((bf16[2,4,8,256]{3,2,1,0:T(8,128)(2,1)S(1)}, bf16[2,4,8,256]{3,2,1,0:T(8,128)(2,1)S(1)}, u32[]{:S(2)}, u32[]{:S(2)}) %collective-permute-start.6) | collective-permute-done | bytes 32800 | tf_op jit(solution)/shard_map/ppermute | solution.py:124
  26.1 0.3 fusion.11
  27.2 0.3 fusion.9
  27.5 0.3 fusion.67
  28.1 3.4 %collective-permute-start.8 = (bf16[8,4,1,256]{3,2,1,0:T(2,128)(2,1)S(1)}, bf16[8,4,1,256]{3,2,1,0:T(2,128)(2,1)S(1)}, u32[]{:S(2)}, u32[]{:S(2)}) collective-permute-start(bf16[8,4,1,256]{3,2,1,0:T(2,128)(2,1)S(1)} %get-tuple-element.30), channel_id=1, source_target_pairs={{8,0},{16,8},{24,16},{9,1},{17,9},{25,17},{10,2},{18,10},{26,18},{... | collective-permute-start | bytes 49160 | tf_op jit(solution)/shard_map/ppermute | solution.py:18
  31.5 1.9 %collective-permute-start.7 = (bf16[8,4,1,256]{3,2,1,0:T(2,128)(2,1)S(1)}, bf16[8,4,1,256]{3,2,1,0:T(2,128)(2,1)S(1)}, u32[]{:S(2)}, u32[]{:S(2)}) collective-permute-start(bf16[8,4,1,256]{3,2,1,0:T(2,128)(2,1)S(1)} %get-tuple-element.29), channel_id=1, source_target_pairs={{0,8},{8,16},{16,24},{1,9},{9,17},{17,25},{2,10},{10,18},{18,26},{... | collective-permute-start | bytes 49160 | tf_op jit(solution)/shard_map/ppermute | solution.py:16
  33.6 3.7 %collective-permute-done.7 = bf16[8,4,1,256]{3,2,1,0:T(2,128)(2,1)S(1)} collective-permute-done((bf16[8,4,1,256]{3,2,1,0:T(2,128)(2,1)S(1)}, bf16[8,4,1,256]{3,2,1,0:T(2,128)(2,1)S(1)}, u32[]{:S(2)}, u32[]{:S(2)}) %collective-permute-start.7) | collective-permute-done | bytes 16416 | tf_op jit(solution)/shard_map/ppermute | solution.py:16
  37.4 6.8 %collective-permute-start.9 = (bf16[8,1,10,256]{3,2,1,0:T(8,128)(2,1)S(1)}, bf16[8,1,10,256]{3,2,1,0:T(8,128)(2,1)S(1)}, u32[]{:S(2)}, u32[]{:S(2)}) collective-permute-start(bf16[8,1,10,256]{3,2,1,0:T(8,128)(2,1)S(1)} %get-tuple-element.25), channel_id=1, source_target_pairs={{0,1},{1,2},{2,3},{3,4},{4,5},{5,6},{6,7},{8,9},{9,10},{10,11},{11... | collective-permute-start | bytes 122888 | tf_op jit(solution)/shard_map/ppermute | solution.py:16
  44.2 1.9 %collective-permute-start.10 = (bf16[8,1,10,256]{3,2,1,0:T(8,128)(2,1)S(1)}, bf16[8,1,10,256]{3,2,1,0:T(8,128)(2,1)S(1)}, u32[]{:S(2)}, u32[]{:S(2)}) collective-permute-start(bf16[8,1,10,256]{3,2,1,0:T(8,128)(2,1)S(1)} %get-tuple-element.26), channel_id=1, source_target_pairs={{1,0},{2,1},{3,2},{4,3},{5,4},{6,5},{7,6},{9,8},{10,9},{11,10},{12... | collective-permute-start | bytes 122888 | tf_op jit(solution)/shard_map/ppermute | solution.py:18
  46.3 3.5 %collective-permute-done.10 = bf16[8,1,10,256]{3,2,1,0:T(8,128)(2,1)S(1)} collective-permute-done((bf16[8,1,10,256]{3,2,1,0:T(8,128)(2,1)S(1)}, bf16[8,1,10,256]{3,2,1,0:T(8,128)(2,1)S(1)}, u32[]{:S(2)}, u32[]{:S(2)}) %collective-permute-start.10) | collective-permute-done | bytes 40992 | tf_op jit(solution)/shard_map/ppermute | solution.py:18
  49.8 0.3 maximum_maximum_fusion
  50.6 0.2 convolution_add_fusion.5
  51.2 0.2 fusion.1
  51.6 0.8 %fusion.6 = bf16[256,256]{1,0:T(8,128)(2,1)} fusion(f32[256,256]{1,0:T(8,128)S(1)} %convolution_add_fusion.1, bf16[256,256]{1,0:T(8,128)(2,1)S(1)} %bitcast.191, bf16[3,3,256,256]{3,2,1,0:T(8,128)(2,1)S(1)} %copy-done.3), kind=kOutput, calls=%fused_computation.27 | convolution fusion | flops 33685504 | bytes 655360 | tf_op jit(solution)/shard_map/dot_general | solution.py:31
  (72 shorter events, 6.0 us)
Async XLA Ops:
  0.0 26.5 %copy-start = (bf16[256,256]{1,0:T(8,128)(2,1)S(1)}, bf16[256,256]{1,0:T(8,128)(2,1)}, u32[]{:S(2)}) copy-start(bf16[256,256]{1,0:T(8,128)(2,1)} %param.18) | copy-start | bytes 393220
  0.0 8.7 %copy-start.2 = (bf16[3,3,256,256]{3,2,1,0:T(8,128)(2,1)S(1)}, bf16[3,3,256,256]{3,2,1,0:T(8,128)(2,1)}, u32[]{:S(2)}) copy-start(bf16[3,3,256,256]{3,2,1,0:T(8,128)(2,1)} %param.12) | copy-start | bytes 3538948
  0.9 5.7 %collective-permute-start.1 = (bf16[2,1,32,256]{3,2,1,0:T(8,128)(2,1)S(1)}, bf16[2,1,32,256]{3,2,1,0:T(8,128)(2,1)S(1)}, u32[]{:S(2)}, u32[]{:S(2)}) collective-permute-start(bf16[2,1,32,256]{3,2,1,0:T(8,128)(2,1)S(1)} %get-tuple-element.42), channel_id=1, source_target_pairs={{1,0},{2,1},{3,2},{4,3},{5,4},{6,5},{7,6},{9,8},{10,9},{11,10},{12... | collective-permute-start | bytes 98312 | tf_op jit(solution)/shard_map/ppermute | solution.py:18
  3.5 4.1 %collective-permute-start = (bf16[2,1,32,256]{3,2,1,0:T(8,128)(2,1)S(1)}, bf16[2,1,32,256]{3,2,1,0:T(8,128)(2,1)S(1)}, u32[]{:S(2)}, u32[]{:S(2)}) collective-permute-start(bf16[2,1,32,256]{3,2,1,0:T(8,128)(2,1)S(1)} %get-tuple-element.41), channel_id=1, source_target_pairs={{0,1},{1,2},{2,3},{3,4},{4,5},{5,6},{6,7},{8,9},{9,10},{10,11},{11... | collective-permute-start | bytes 98312 | tf_op jit(solution)/shard_map/ppermute | solution.py:16
  8.6 0.9 %copy-start.1 = (bf16[2,4,32,256]{3,2,1,0:T(8,128)(2,1)S(1)}, bf16[2,4,32,256]{3,2,1,0:T(8,128)(2,1)}, u32[]{:S(2)}) copy-start(bf16[2,4,32,256]{3,2,1,0:T(8,128)(2,1)} %param.11) | copy-start | bytes 393220
  10.9 7.5 %copy-start.4 = (bf16[3,3,256,256]{3,2,1,0:T(8,128)(2,1)S(1)}, bf16[3,3,256,256]{3,2,1,0:T(8,128)(2,1)}, u32[]{:S(2)}) copy-start(bf16[3,3,256,256]{3,2,1,0:T(8,128)(2,1)} %param.13) | copy-start | bytes 3538948
  11.0 6.3 %collective-permute-start.3 = (bf16[2,1,32,256]{3,2,1,0:T(8,128)(2,1)S(1)}, bf16[2,1,32,256]{3,2,1,0:T(8,128)(2,1)S(1)}, u32[]{:S(2)}, u32[]{:S(2)}) collective-permute-start(bf16[2,1,32,256]{3,2,1,0:T(8,128)(2,1)S(1)} %get-tuple-element.38), channel_id=1, source_target_pairs={{1,0},{2,1},{3,2},{4,3},{5,4},{6,5},{7,6},{9,8},{10,9},{11,10},{12... | collective-permute-start | bytes 98312 | tf_op jit(solution)/shard_map/ppermute | solution.py:18
  14.2 4.1 %collective-permute-start.2 = (bf16[2,1,32,256]{3,2,1,0:T(8,128)(2,1)S(1)}, bf16[2,1,32,256]{3,2,1,0:T(8,128)(2,1)S(1)}, u32[]{:S(2)}, u32[]{:S(2)}) collective-permute-start(bf16[2,1,32,256]{3,2,1,0:T(8,128)(2,1)S(1)} %get-tuple-element.37), channel_id=1, source_target_pairs={{0,1},{1,2},{2,3},{3,4},{4,5},{5,6},{6,7},{8,9},{9,10},{10,11},{11... | collective-permute-start | bytes 98312 | tf_op jit(solution)/shard_map/ppermute | solution.py:16
  19.9 1.8 %copy-start.9 = (f32[8,8]{1,0:T(8,128)S(1)}, f32[8,8]{1,0:T(8,128)}, u32[]{:S(2)}) copy-start(f32[8,8]{1,0:T(8,128)} %param.20) | copy-start | bytes 772
  20.1 5.6 %copy-start.5 = (bf16[3,256,256]{2,1,0:T(8,128)(2,1)S(1)}, bf16[3,256,256]{2,1,0:T(8,128)(2,1)}, u32[]{:S(2)}) copy-start(bf16[3,256,256]{2,1,0:T(8,128)(2,1)} %param.14) | copy-start | bytes 1179652
  20.4 6.0 %copy-start.10 = (f32[256]{0:T(256)S(1)}, f32[256]{0:T(256)}, u32[]{:S(2)}) copy-start(f32[256]{0:T(256)} %param.15) | copy-start | bytes 3076
  20.5 2.8 %collective-permute-start.4 = (bf16[2,4,8,256]{3,2,1,0:T(8,128)(2,1)S(1)}, bf16[2,4,8,256]{3,2,1,0:T(8,128)(2,1)S(1)}, u32[]{:S(2)}, u32[]{:S(2)}) collective-permute-start(bf16[2,4,8,256]{3,2,1,0:T(8,128)(2,1)S(1)} %get-tuple-element.33), channel_id=1, source_target_pairs={{0,8},{8,0},{16,24},{24,16},{1,9},{9,1},{17,25},{25,17},{2,10},{10... | collective-permute-start | bytes 98312 | tf_op jit(solution)/shard_map/ppermute | solution.py:124
  21.8 3.1 %collective-permute-start.5 = (bf16[2,4,8,256]{3,2,1,0:T(8,128)(2,1)S(1)}, bf16[2,4,8,256]{3,2,1,0:T(8,128)(2,1)S(1)}, u32[]{:S(2)}, u32[]{:S(2)}) collective-permute-start(bf16[2,4,8,256]{3,2,1,0:T(8,128)(2,1)S(1)} %get-tuple-element.32), channel_id=1, source_target_pairs={{0,16},{8,24},{16,0},{24,8},{1,17},{9,25},{17,1},{25,9},{2,18},{10... | collective-permute-start | bytes 98312 | tf_op jit(solution)/shard_map/ppermute | solution.py:124
  22.0 3.7 %collective-permute-start.6 = (bf16[2,4,8,256]{3,2,1,0:T(8,128)(2,1)S(1)}, bf16[2,4,8,256]{3,2,1,0:T(8,128)(2,1)S(1)}, u32[]{:S(2)}, u32[]{:S(2)}) collective-permute-start(bf16[2,4,8,256]{3,2,1,0:T(8,128)(2,1)S(1)} %get-tuple-element.31), channel_id=1, source_target_pairs={{0,24},{8,16},{16,8},{24,0},{1,25},{9,17},{17,9},{25,1},{2,26},{10... | collective-permute-start | bytes 98312 | tf_op jit(solution)/shard_map/ppermute | solution.py:124
  25.9 0.9 %copy-start.6 = (bf16[256,256]{1,0:T(8,128)(2,1)S(1)}, bf16[256,256]{1,0:T(8,128)(2,1)}, u32[]{:S(2)}) copy-start(bf16[256,256]{1,0:T(8,128)(2,1)} %param.17) | copy-start | bytes 393220
  25.9 1.1 %copy-start.7 = (bf16[256,256]{1,0:T(8,128)(2,1)S(1)}, bf16[256,256]{1,0:T(8,128)(2,1)}, u32[]{:S(2)}) copy-start(bf16[256,256]{1,0:T(8,128)(2,1)} %param.16) | copy-start | bytes 393220
  26.8 1.0 %copy-start.8 = (bf16[256,256]{1,0:T(8,128)(2,1)S(1)}, bf16[256,256]{1,0:T(8,128)(2,1)}, u32[]{:S(2)}) copy-start(bf16[256,256]{1,0:T(8,128)(2,1)} %param.19) | copy-start | bytes 393220
  27.2 6.2 %copy-start.3 = (bf16[3,3,256,256]{3,2,1,0:T(8,128)(2,1)S(1)}, bf16[3,3,256,256]{3,2,1,0:T(8,128)(2,1)}, u32[]{:S(2)}) copy-start(bf16[3,3,256,256]{3,2,1,0:T(8,128)(2,1)} %param.21) | copy-start | bytes 3538948
  28.1 5.6 %collective-permute-start.8 = (bf16[8,4,1,256]{3,2,1,0:T(2,128)(2,1)S(1)}, bf16[8,4,1,256]{3,2,1,0:T(2,128)(2,1)S(1)}, u32[]{:S(2)}, u32[]{:S(2)}) collective-permute-start(bf16[8,4,1,256]{3,2,1,0:T(2,128)(2,1)S(1)} %get-tuple-element.30), channel_id=1, source_target_pairs={{8,0},{16,8},{24,16},{9,1},{17,9},{25,17},{10,2},{18,10},{26,18},{... | collective-permute-start | bytes 49160 | tf_op jit(solution)/shard_map/ppermute | solution.py:18
  31.5 5.8 %collective-permute-start.7 = (bf16[8,4,1,256]{3,2,1,0:T(2,128)(2,1)S(1)}, bf16[8,4,1,256]{3,2,1,0:T(2,128)(2,1)S(1)}, u32[]{:S(2)}, u32[]{:S(2)}) collective-permute-start(bf16[8,4,1,256]{3,2,1,0:T(2,128)(2,1)S(1)} %get-tuple-element.29), channel_id=1, source_target_pairs={{0,8},{8,16},{16,24},{1,9},{9,17},{17,25},{2,10},{10,18},{18,26},{... | collective-permute-start | bytes 49160 | tf_op jit(solution)/shard_map/ppermute | solution.py:16
  37.4 8.9 %collective-permute-start.9 = (bf16[8,1,10,256]{3,2,1,0:T(8,128)(2,1)S(1)}, bf16[8,1,10,256]{3,2,1,0:T(8,128)(2,1)S(1)}, u32[]{:S(2)}, u32[]{:S(2)}) collective-permute-start(bf16[8,1,10,256]{3,2,1,0:T(8,128)(2,1)S(1)} %get-tuple-element.25), channel_id=1, source_target_pairs={{0,1},{1,2},{2,3},{3,4},{4,5},{5,6},{6,7},{8,9},{9,10},{10,11},{11... | collective-permute-start | bytes 122888 | tf_op jit(solution)/shard_map/ppermute | solution.py:16
  44.2 5.6 %collective-permute-start.10 = (bf16[8,1,10,256]{3,2,1,0:T(8,128)(2,1)S(1)}, bf16[8,1,10,256]{3,2,1,0:T(8,128)(2,1)S(1)}, u32[]{:S(2)}, u32[]{:S(2)}) collective-permute-start(bf16[8,1,10,256]{3,2,1,0:T(8,128)(2,1)S(1)} %get-tuple-element.26), channel_id=1, source_target_pairs={{1,0},{2,1},{3,2},{4,3},{5,4},{6,5},{7,6},{9,8},{10,9},{11,10},{12... | collective-permute-start | bytes 122888 | tf_op jit(solution)/shard_map/ppermute | solution.py:18
